TPU v7x, 128 devices: a whole 4x4x4 slice. The times are simulated.
128 devices in a mesh: dp: 32 (over x, z, core), rep: 4 (over y).
Axes of the slice: x: 4, y: 4, z: 4, core: 2. Of those that a mesh axis runs over, the one named last changes fastest.
Arguments:
- cross_in: bfloat16 [65536, 3456], P(('dp', 'rep')), may hold values from -24 to 24
- cotangent: bfloat16 [65536, 3456], P(('dp', 'rep')), may hold values from -24 to 24
- weight_down: bfloat16 [3456, 512], replicated, may hold values from -0.109375 to 0.109375
- weight_up: bfloat16 [512, 3456], replicated, may hold values from -0.25 to 0.25
- cross_bias: float32 [3456], replicated, may hold values from -3 to 3
- row_place: int32 [65536, 26], P(('dp', 'rep')), may hold values from 0 to 66559, as said below
- frequent_table: float32 [1024, 128], replicated, may hold values from -0.6 to 0.6
- frequent_accum: float32 [1024], replicated, may hold values from 416 to 106496
- shard_table: float32 [65536, 128], P('dp'), may hold values from -0.6 to 0.6
- shard_accum: float32 [65536], P('dp'), may hold values from 0.01 to 1
Outputs:
- new_frequent: float32 [1024, 128], replicated
- new_frequent_accum: float32 [1024], replicated
- new_shard: float32 [65536, 128], P('dp')
- new_shard_accum: float32 [65536], P('dp')
- grad_up: float32 [512, 3456], P(('dp', 'rep'))
- grad_down: float32 [3456, 512], P(('dp', 'rep'))
- grad_bias: float32 [3456], P(('dp', 'rep'))
Inputs may be any that keep to these rules, and one draw needn't show every extreme that they name: `row_place`: within the rows of one device (aligned blocks of 512 samples), at most 208 entries name rows of any one owner, and in every block some owner is named by exactly 208 entries; every owner is named at least once in every block.
All inputs are finite; a program needn't handle non-finite values.
Results may differ from a plain program's by a relative error of at most 0.0013.
The roundings to bfloat16 on the way count: a program that leaves them out, or rounds other values in their place, can miss the bound.
Values sent between devices are 32-bit elements; how exact they have to be, the bound alone decides.
A program may use at most 192 MiB of HBM per device.

v0:
```python
import jax
import jax.numpy as jnp
from jax import lax
from jax.sharding import PartitionSpec as P

learn_rate = 0.05
eps_ada = 1e-08


def row_adagrad(table, accum, grad):
    accum_new = accum + jnp.mean(grad * grad, axis=1)
    return (table - learn_rate * grad / (jnp.sqrt(accum_new)[:, None] + eps_ada), accum_new)


def body(
    cross_in,
    cotangent,
    weight_down,
    weight_up,
    cross_bias,
    row_place,
    frequent_table,
    frequent_accum,
    shard_table,
    shard_accum,
):
    emb_width = frequent_table.shape[1]
    num_tables = row_place.shape[1]
    local_rows = cross_in.shape[0]
    f_count = frequent_table.shape[0]
    owned_rows = shard_table.shape[0]
    hidden = jnp.dot(cross_in, weight_down, preferred_element_type=jnp.float32).astype(jnp.bfloat16)
    scaled = jnp.dot(hidden, weight_up, preferred_element_type=jnp.float32) + cross_bias
    cot_wide = cotangent.astype(jnp.float32)
    inner = cot_wide * cross_in.astype(jnp.float32)
    inner_half = inner.astype(jnp.bfloat16)
    back_low = lax.dot_general(
        inner_half, weight_up, (((1,), (1,)), ((), ())), preferred_element_type=jnp.float32
    ).astype(jnp.bfloat16)
    back_in = cot_wide * (scaled + 1.0) + lax.dot_general(
        back_low, weight_down, (((1,), (1,)), ((), ())), preferred_element_type=jnp.float32
    )
    local_up = lax.dot_general(
        hidden, inner_half, (((0,), (0,)), ((), ())), preferred_element_type=jnp.float32
    )
    local_down = lax.dot_general(
        cross_in, back_low, (((0,), (0,)), ((), ())), preferred_element_type=jnp.float32
    )
    local_bias = jnp.sum(inner, axis=0)
    grad_up, grad_down, grad_bias = (
        lax.psum_scatter(local_up, ("dp", "rep"), scatter_dimension=0, tiled=True),
        lax.psum_scatter(local_down, ("dp", "rep"), scatter_dimension=0, tiled=True),
        lax.psum_scatter(local_bias, ("dp", "rep"), scatter_dimension=0, tiled=True),
    )
    values = back_in[:, emb_width:].reshape(local_rows * num_tables, emb_width)
    places = row_place.reshape(-1)
    is_frequent = places < f_count
    freq_grad = jax.ops.segment_sum(values, jnp.where(is_frequent, places, f_count), f_count + 1)[
        :f_count
    ]
    shards = lax.axis_size("dp")
    capacity = local_rows * num_tables // (2 * shards)
    owners = jnp.where(is_frequent, shards, (places - f_count) // owned_rows)
    owner_row = jnp.where(is_frequent, 0, (places - f_count) % owned_rows)
    sorted_order = jnp.argsort(owners, stable=True)
    sorted_owner = owners[sorted_order]
    counts = jnp.sum((owners[:, None] == jnp.arange(shards + 1)[None, :]).astype(jnp.int32), axis=0)
    starts = jnp.cumsum(counts) - counts
    slot_pos = jnp.arange(owners.shape[0]) - starts[sorted_owner]
    target = jnp.where(sorted_owner < shards, sorted_owner * capacity + slot_pos, shards * capacity)
    bucket = (
        jnp.zeros((shards * capacity + 1, emb_width), jnp.float32)
        .at[target]
        .set(values[sorted_order])
    )
    bucket = bucket[: shards * capacity].reshape(shards, capacity, emb_width)
    bucket_rows = (
        jnp.zeros((shards * capacity + 1,), jnp.int32).at[target].set(owner_row[sorted_order])
    )
    bucket_rows = bucket_rows[: shards * capacity].reshape(shards, capacity)
    arrived, arrived_rows = (
        lax.all_to_all(bucket, "dp", split_axis=0, concat_axis=0, tiled=True),
        lax.all_to_all(bucket_rows, "dp", split_axis=0, concat_axis=0, tiled=True),
    )
    shard_grad = jax.ops.segment_sum(
        arrived.reshape(-1, emb_width), arrived_rows.reshape(-1), owned_rows
    )
    shard_grad = lax.psum(shard_grad, "rep")
    new_shard, new_shard_accum = row_adagrad(shard_table, shard_accum, shard_grad)
    freq_total = lax.psum(freq_grad, ("dp", "rep"))
    new_frequent, new_frequent_accum = row_adagrad(frequent_table, frequent_accum, freq_total)
    return (
        new_frequent,
        new_frequent_accum,
        new_shard,
        new_shard_accum,
        grad_up,
        grad_down,
        grad_bias,
    )


def solution(mesh):
    in_specs = (
        P(("dp", "rep"), None),
        P(("dp", "rep"), None),
        P(),
        P(),
        P(),
        P(("dp", "rep"), None),
        P(),
        P(),
        P("dp", None),
        P("dp"),
    )
    out_specs = (
        P(),
        P(),
        P("dp", None),
        P("dp"),
        P(("dp", "rep"), None),
        P(("dp", "rep"), None),
        P(("dp", "rep")),
    )
    return jax.shard_map(body, mesh=mesh, in_specs=in_specs, out_specs=out_specs, check_vma=False)
```

profile of v0, /device:TPU:1, one launch (start us, length us, event | category | flops | bytes accessed | tf_op | source)
XLA Modules:
  0.0 876.3 jit_solution(13880018079292635862)
XLA Ops:
  7.2 1.6 broadcast_add_fusion
  9.7 1.7 copy.31
  11.3 1.8 sub.33
  14.9 1.5 fusion.18
  18.1 1.4 reduce-window.9
  22.4 9.1 %sort.17 = (s32[13312]{0:T(1024)}, s32[13312]{0:T(1024)}) sort(s32[13312]{0:T(1024)} %copy-done.2, s32[13312]{0:T(1024)} %iota.12), dimensions={0}, to_apply=%region_3.0 | sort | flops 186368 | bytes 212992 | tf_op jit(solution)/shard_map/jit(argsort)/sort | solution.py:65
  31.5 1.4 fusion.19
  32.9 121.2 %gather_fusion = s32[13312]{0:T(1024)} fusion(s32[13312]{0:T(1024)} %copy-done.2, s32[13312]{0:T(1024)} %fusion.19), kind=kCustom, calls=%fused_computation | custom fusion | bytes 159744 | tf_op jit(solution)/shard_map/gather | solution.py:66
  154.1 5.3 compare_select_fusion.3
  159.4 4.2 compare_reduce_fusion.25
  163.7 16.6 %select_select_fusion = s32[13312]{0:T(1024)S(1)} fusion(pred[13312]{0:T(1024)(128)(4,1)S(1)} %get-tuple-element.62, pred[13312]{0:T(1024)(128)(4,1)S(1)} %get-tuple-element.61, pred[13312]{0:T(1024)(128)(4,1)S(1)} %get-tuple-element.60, pred[13312]{0:T(1024)(128)(4,1)S(1)} %get-tuple-element.59, pred[13312]{0:T(1024)(128)(4,1)S(1)} %get-tuple-element.58, ...), kind=kLoop, calls=%fused_computation.77 | loop fusion | flops 346112 | bytes 452712 | tf_op jit(solution)/shard_map/gather | solution.py:69
  180.3 1.6 compare_select_fusion
  181.8 120.7 %gather_fusion.1 = s32[13312]{0:T(1024)} fusion(s32[13312]{0:T(1024)} %get-tuple-element.72, s32[13312]{0:T(1024)} %fusion.19), kind=kCustom, calls=%fused_computation.1 | custom fusion | bytes 159744 | tf_op jit(solution)/shard_map/gather | solution.py:78
  302.6 49.8 %scatter_custom_fusion.1 = s32[6657]{0:T(1024)} fusion(s32[13312]{0:T(1024)} %bitcast.62, s32[13312]{0:T(1024)} %gather_fusion.1, s32[]{:T(128)} %constant.29.clone.1), kind=kCustom, calls=%fused_computation.83 | custom fusion | bytes 27140 | tf_op jit(solution)/shard_map/scatter | solution.py:78
  352.4 1.5 all_to_all.9
  353.9 9.8 %all-to-all-start = ((s32[32,1,208]{2,1,0:T(1,128)}), s32[32,1,208]{2,1,0:T(1,128)}, u32[]{:S(2)}, u32[]{:S(2)}) async-start(s32[32,1,208]{2,1,0:T(1,128)} %all_to_all.9), calls=%async_computation | async-start | bytes 65536 | tf_op jit(solution)/shard_map/all_to_all | solution.py:83
  363.7 2.6 convert_element_type.18
  367.9 2.0 convolution_convert_fusion
  369.9 2.1 fusion.10
  372.1 2.1 fusion.26
  374.3 2.1 fusion.27
  376.4 3.3 slice_add_fusion
  379.7 7.8 reshape.231
  387.5 108.6 %scatter_custom_fusion.2 = f32[6657,128]{1,0:T(8,128)S(1)} fusion(s32[13312]{0:T(1024)} %bitcast.63, f32[13312,128]{1,0:T(8,128)} %reshape.231, s32[13312]{0:T(1024)} %fusion.19, f32[]{:T(128)} %constant.21.clone.1), kind=kCustom, calls=%fused_computation.12 | custom fusion | bytes 3408896 | tf_op jit(solution)/shard_map/scatter | solution.py:74
  496.1 2.1 slice.62
  498.2 7.8 all-to-all-start.1
  506.1 1.7 copy.29
  507.8 1.8 reshape.157
  509.6 1.5 compare_select_fusion.2
  511.1 72.4 %scatter_custom_fusion = f32[1025,128]{1,0:T(8,128)} fusion(s32[13312]{0:T(1024)} %bitcast.64, f32[13312,128]{1,0:T(8,128)} %reshape.231, f32[]{:T(128)} %constant.21.clone.1), kind=kCustom, calls=%fused_computation.33 | custom fusion | flops 1703936 | bytes 525312 | tf_op jit(solution)/shard_map/scatter-add | solution.py:58
  583.4 1.9 slice.60
  585.3 1.4 reduce.27
  586.8 1.5 reshape.253
  588.2 41.0 %scatter_custom_fusion.3 = f32[2048,128]{1,0:T(8,128)} fusion(s32[6656]{0:T(1024)} %reshape.253, f32[6656,128]{1,0:T(8,128)} %bitcast.40, f32[]{:T(128)} %constant.21.clone.1), kind=kCustom, calls=%fused_computation.26 | custom fusion | flops 851968 | bytes 1049088 | tf_op jit(solution)/shard_map/scatter-add | solution.py:85
  629.4 6.2 convolution_bitcast_fusion
  635.6 5.1 fusion.6
  640.7 4.2 fusion.3
  644.8 67.5 %all-reduce.2 = f32[3456]{0:T(1024)} all-reduce(f32[3456]{0:T(1024)S(1)} %fusion.3), channel_id=4, replica_groups=mesh['dp'=32,'rep'=4] {'dp','rep'}, use_global_device_ids=true, to_apply=%region_14.15.clone | all-reduce | flops 3456 | bytes 27648
  712.3 1.3 dynamic-slice.2
  713.6 1.6 multiply_reduce_fusion
  715.2 1.3 sqrt_add_fusion
  716.5 3.0 divide_subtract_fusion
  719.4 140.0 %all-reduce.9.cloned.1.call-done = (f32[1024,128]{1,0:T(8,128)}, f32[512,3456]{1,0:T(8,128)}, f32[3456,512]{0,1:T(8,128)}) async-done(((f32[1024,128]{1,0:T(8,128)}, f32[512,3456]{1,0:T(8,128)}, f32[3456,512]{0,1:T(8,128)}), (f32[1024,128]{1,0:T(8,128)}, f32[512,3456]{1,0:T(8,128)}, f32[3456,512]{0,1:T(8,128)})) %all-reduce.9.cloned.1.call-update) | async-done | bytes 14680080 | tf_op jit(solution)/shard_map/psum | solution.py:90
  860.7 1.9 constant_dynamic-slice_fusion
  862.6 1.7 copy.33
  864.3 1.3 sqrt_add_fusion.1
  865.5 2.2 divide_subtract_fusion.1
  867.7 1.5 constant_dynamic-slice_fusion.1
  (45 shorter events, 10.3 us)
Async XLA Ops:
  7.2 362.8 %copy-start = (bf16[512,3456]{1,0:T(8,128)(2,1)S(1)}, bf16[512,3456]{1,0:T(8,128)(2,1)}, u32[]{:S(2)}) copy-start(bf16[512,3456]{1,0:T(8,128)(2,1)} %param.13) | copy-start | bytes 10616836
  16.4 0.6 copy-start.2
  353.9 144.3 %all-to-all-start = ((s32[32,1,208]{2,1,0:T(1,128)}), s32[32,1,208]{2,1,0:T(1,128)}, u32[]{:S(2)}, u32[]{:S(2)}) async-start(s32[32,1,208]{2,1,0:T(1,128)} %all_to_all.9), calls=%async_computation | async-start | bytes 65536 | tf_op jit(solution)/shard_map/all_to_all | solution.py:83
  363.7 3.1 copy-start.3
  363.7 4.1 copy-start.7
  367.9 2.1 copy-start.5
  369.9 2.1 copy-start.9
  372.1 4.3 copy-start.11
  372.1 2.2 copy-start.8
  374.3 2.1 copy-start.12
  498.2 131.1 %copy-start.4 = (bf16[512,3456]{1,0:T(8,128)(2,1)S(1)}, bf16[512,3456]{1,0:T(8,128)(2,1)}, u32[]{:S(2)}) copy-start(bf16[512,3456]{1,0:T(8,128)(2,1)} %param.10) | copy-start | bytes 10616836
  498.2 90.0 %all-to-all-start.1 = ((f32[32,208,128]{2,1,0:T(8,128)}), f32[32,208,128]{2,1,0:T(8,128)}, u32[]{:S(2)}, u32[]{:S(2)}) async-start(f32[32,208,128]{2,1,0:T(8,128)} %bitcast.56), calls=%async_computation.1 | async-start | bytes 6815744 | tf_op jit(solution)/shard_map/all_to_all | solution.py:82
  506.1 207.5 %all-reduce.7.cloned.1.call-start = ((), (), s32[]{:S(2)}) async-start(), calls=%async_computation.2 | async-start | bytes 2097152 | tf_op jit(solution)/shard_map/psum | solution.py:88
  629.3 230.1 %all-reduce.9.cloned.1.call-start = ((), (), s32[]{:S(2)}) async-start(), calls=%async_computation.3 | async-start | bytes 29360128 | tf_op jit(solution)/shard_map/psum | solution.py:90
  629.3 6.2 copy-start.6
  629.4 6.2 copy-start.10
  640.7 228.6 %copy-start.1 = (bf16[512,3456]{1,0:T(8,128)(2,1)S(1)}, bf16[512,3456]{1,0:T(8,128)(2,1)}, u32[]{:S(2)}) copy-start(bf16[512,3456]{1,0:T(8,128)(2,1)} %param.13) | copy-start | bytes 10616836
Sparse Core Ops, SparseCore 0:
  629.4 46.4 all-reduce.6
  683.0 176.4 all-reduce.8
where the time goes:
time: 884 us; the launch traced here: 876 us
  local copies, waits for them, and re-layouts  435 us (49%)
  other arithmetic  182 us (21%)
  waiting for transfers between devices  140 us (16%)
  blocking collectives  67.5 us (8%)
  matrix products  19.6 us (2%)
  starting transfers between devices  17.8 us (2%)
  between operations  14.5 us (2%)
    psum x1, waiting for transfers between devices, body(): freq_total = lax.psum(freq_grad, ('dp', 'rep'))  140 us
    gather x1, local copies, waits for them, and re-layouts, body(): sorted_owner = owners[sorted_order]  121 us
    gather x1, local copies, waits for them, and re-layouts, body(): owner_row[sorted_order]  121 us
    scatter x1, local copies, waits for them, and re-layouts, body(): bucket = jnp.zeros((shards * capacity + 1, emb_width), jnp.float32).at[ta...  109 us
    scatter-add x1, other arithmetic, body(): jax.ops.segment_sum(values, jnp.where(is_frequent, places, f_count), f_co...  72.4 us
    unnamed x1, blocking collectives  67.5 us
    scatter x1, local copies, waits for them, and re-layouts, body(): jnp.zeros((shards * capacity + 1,), jnp.int32).at[target]  49.8 us
    scatter-add x1, other arithmetic, body(): jax.ops.segment_sum(arrived.reshape(-1, emb_width), arrived_rows.reshape(...  41 us
  transfers between devices with their start and end apart: 4, of which 1 were waited for; matrix products, arithmetic and copies ran while one was open for 27% of the time, Pallas kernels for 0%

commit v1 on v0

--- a/solution.py
+++ b/solution.py
@@ -87,7 +87,8 @@
     )
     shard_grad = lax.psum(shard_grad, "rep")
     new_shard, new_shard_accum = row_adagrad(shard_table, shard_accum, shard_grad)
-    freq_total = lax.psum(freq_grad, ("dp", "rep"))
+    group_cards = lambda patch: lax.psum(lax.psum(patch, "dp"), "rep")
+    freq_total = group_cards(freq_grad)
     new_frequent, new_frequent_accum = row_adagrad(frequent_table, frequent_accum, freq_total)
     return (
         new_frequent,

time: 884 us -> 943 us (1.067)
  waiting for transfers between devices: 140 us -> 199 us
    unnamed x2 -> x4, waiting for transfers between devices: 0.03 us -> 138 us
    psum x2, waiting for transfers between devices: 140 us -> 61 us  [body(): group_cards = lambda patch: lax.psum(lax.psum(patch, 'dp'), 'rep')]
  transfers between devices with their start and end apart: 4 -> 5, of which waited for: 1 -> 2; matrix products, arithmetic and copies ran while one was open for 27% -> 30% of each run, Pallas kernels for 0% -> 0%
where the time goes in v1:
time: 943 us; the launch traced here: 934 us
  local copies, waits for them, and re-layouts  435 us (46%)
  waiting for transfers between devices  199 us (21%)
  other arithmetic  182 us (19%)
  blocking collectives  66.6 us (7%)
  matrix products  19.6 us (2%)
  starting transfers between devices  17.8 us (2%)
  between operations  14.2 us (2%)
    unnamed x4, waiting for transfers between devices  138 us
    gather x1, local copies, waits for them, and re-layouts, body(): sorted_owner = owners[sorted_order]  121 us
    gather x1, local copies, waits for them, and re-layouts, body(): owner_row[sorted_order]  121 us
    scatter x1, local copies, waits for them, and re-layouts, body(): bucket = jnp.zeros((shards * capacity + 1, emb_width), jnp.float32).at[ta...  109 us
    scatter-add x1, other arithmetic, body(): jax.ops.segment_sum(values, jnp.where(is_frequent, places, f_count), f_co...  72.4 us
    unnamed x1, blocking collectives  66.6 us
    psum x2, waiting for transfers between devices, body(): group_cards = lambda patch: lax.psum(lax.psum(patch, 'dp'), 'rep')  61 us
    scatter x1, local copies, waits for them, and re-layouts, body(): jnp.zeros((shards * capacity + 1,), jnp.int32).at[target]  49.8 us
  transfers between devices with their start and end apart: 5, of which 2 were waited for; matrix products, arithmetic and copies ran while one was open for 30% of the time, Pallas kernels for 0%

profile of v1, /device:TPU:1, one launch (start us, length us, event | category | flops | bytes accessed | tf_op | source)
XLA Modules:
  0.0 934.4 jit_solution(16993837803218732902)
XLA Ops:
  7.2 1.6 broadcast_add_fusion
  9.7 1.7 copy.31
  11.3 1.8 sub.33
  14.9 1.5 fusion.18
  18.1 1.4 reduce-window.9
  22.4 9.1 sort.17
  31.5 1.4 fusion.19
  32.9 121.2 %gather_fusion = s32[13312]{0:T(1024)} fusion(s32[13312]{0:T(1024)} %copy-done.2, s32[13312]{0:T(1024)} %fusion.19), kind=kCustom, calls=%fused_computation | custom fusion | bytes 159744 | tf_op jit(solution)/shard_map/gather | solution.py:66
  154.1 5.3 compare_select_fusion.3
  159.4 4.2 compare_reduce_fusion.25
  163.7 16.6 %select_select_fusion = s32[13312]{0:T(1024)S(1)} fusion(pred[13312]{0:T(1024)(128)(4,1)S(1)} %get-tuple-element.62, pred[13312]{0:T(1024)(128)(4,1)S(1)} %get-tuple-element.61, pred[13312]{0:T(1024)(128)(4,1)S(1)} %get-tuple-element.60, pred[13312]{0:T(1024)(128)(4,1)S(1)} %get-tuple-element.59, pred[13312]{0:T(1024)(128)(4,1)S(1)} %get-tuple-element.58, ...), kind=kLoop, calls=%fused_computation.77 | loop fusion | flops 346112 | bytes 452712 | tf_op jit(solution)/shard_map/gather | solution.py:69
  180.3 1.6 compare_select_fusion
  181.8 120.7 %gather_fusion.1 = s32[13312]{0:T(1024)} fusion(s32[13312]{0:T(1024)} %get-tuple-element.73, s32[13312]{0:T(1024)} %fusion.19), kind=kCustom, calls=%fused_computation.1 | custom fusion | bytes 159744 | tf_op jit(solution)/shard_map/gather | solution.py:78
  302.6 49.8 %scatter_custom_fusion.1 = s32[6657]{0:T(1024)} fusion(s32[13312]{0:T(1024)} %bitcast.62, s32[13312]{0:T(1024)} %gather_fusion.1, s32[]{:T(128)} %constant.29.clone.1), kind=kCustom, calls=%fused_computation.83 | custom fusion | bytes 27140 | tf_op jit(solution)/shard_map/scatter | solution.py:78
  352.4 1.5 all_to_all.9
  353.9 9.8 %all-to-all-start = ((s32[32,1,208]{2,1,0:T(1,128)}), s32[32,1,208]{2,1,0:T(1,128)}, u32[]{:S(2)}, u32[]{:S(2)}) async-start(s32[32,1,208]{2,1,0:T(1,128)} %all_to_all.9), calls=%async_computation | async-start | bytes 65536 | tf_op jit(solution)/shard_map/all_to_all | solution.py:83
  363.7 2.6 convert_element_type.18
  367.9 2.0 convolution_convert_fusion
  369.9 2.1 fusion.10
  372.1 2.1 fusion.26
  374.3 2.1 fusion.27
  376.4 3.3 slice_add_fusion
  379.7 7.8 reshape.231
  387.5 108.6 %scatter_custom_fusion.2 = f32[6657,128]{1,0:T(8,128)S(1)} fusion(s32[13312]{0:T(1024)} %bitcast.63, f32[13312,128]{1,0:T(8,128)} %reshape.231, s32[13312]{0:T(1024)} %fusion.19, f32[]{:T(128)} %constant.21.clone.1), kind=kCustom, calls=%fused_computation.12 | custom fusion | bytes 3408896 | tf_op jit(solution)/shard_map/scatter | solution.py:74
  496.1 2.1 slice.62
  498.2 7.8 all-to-all-start.1
  506.1 1.7 copy.29
  507.8 1.8 reshape.157
  509.6 1.5 compare_select_fusion.2
  511.1 72.4 %scatter_custom_fusion = f32[1025,128]{1,0:T(8,128)} fusion(s32[13312]{0:T(1024)} %bitcast.64, f32[13312,128]{1,0:T(8,128)} %reshape.231, f32[]{:T(128)} %constant.21.clone.1), kind=kCustom, calls=%fused_computation.33 | custom fusion | flops 1703936 | bytes 525312 | tf_op jit(solution)/shard_map/scatter-add | solution.py:58
  583.4 1.9 slice.60
  585.4 1.5 reduce.27
  586.8 1.5 reshape.253
  588.3 41.0 %scatter_custom_fusion.3 = f32[2048,128]{1,0:T(8,128)} fusion(s32[6656]{0:T(1024)} %reshape.253, f32[6656,128]{1,0:T(8,128)} %bitcast.40, f32[]{:T(128)} %constant.21.clone.1), kind=kCustom, calls=%fused_computation.26 | custom fusion | flops 851968 | bytes 1049088 | tf_op jit(solution)/shard_map/scatter-add | solution.py:85
  629.3 61.0 %all-reduce.9.cloned.1.call-done = f32[1024,128]{1,0:T(8,128)} async-done(((f32[1024,128]{1,0:T(8,128)}), f32[1024,128]{1,0:T(8,128)}) %all-reduce.9.cloned.1.call-update) | async-done | bytes 524304 | tf_op jit(solution)/shard_map/psum | solution.py:90
  690.5 6.2 convolution_bitcast_fusion
  696.7 5.1 fusion.6
  701.8 4.2 fusion.3
  706.0 66.6 %all-reduce.2 = f32[3456]{0:T(1024)} all-reduce(f32[3456]{0:T(1024)S(1)} %fusion.3), channel_id=4, replica_groups=mesh['dp'=32,'rep'=4] {'dp','rep'}, use_global_device_ids=true, to_apply=%region_15.16.clone | all-reduce | flops 3456 | bytes 27648
  775.2 1.6 multiply_reduce_fusion
  776.8 1.3 sqrt_add_fusion.1
  778.1 1.3 sqrt_add_fusion
  779.4 2.3 divide_subtract_fusion.1
  781.7 3.0 divide_subtract_fusion
  784.7 137.9 %all-reduce.11.cloned.1.call-done = (f32[512,3456]{1,0:T(8,128)}, f32[3456,512]{0,1:T(8,128)}) async-done(((f32[512,3456]{1,0:T(8,128)}, f32[3456,512]{0,1:T(8,128)}), (f32[512,3456]{1,0:T(8,128)}, f32[3456,512]{0,1:T(8,128)})) %all-reduce.11.cloned.1.call-update) | async-done | bytes 14155792
  922.5 1.9 constant_dynamic-slice_fusion
  924.4 1.7 copy.33
  926.1 1.5 constant_dynamic-slice_fusion.1
  (48 shorter events, 11.7 us)
Async XLA Ops:
  7.2 362.8 %copy-start = (bf16[512,3456]{1,0:T(8,128)(2,1)S(1)}, bf16[512,3456]{1,0:T(8,128)(2,1)}, u32[]{:S(2)}) copy-start(bf16[512,3456]{1,0:T(8,128)(2,1)} %param.13) | copy-start | bytes 10616836
  16.4 0.6 copy-start.2
  353.9 144.3 %all-to-all-start = ((s32[32,1,208]{2,1,0:T(1,128)}), s32[32,1,208]{2,1,0:T(1,128)}, u32[]{:S(2)}, u32[]{:S(2)}) async-start(s32[32,1,208]{2,1,0:T(1,128)} %all_to_all.9), calls=%async_computation | async-start | bytes 65536 | tf_op jit(solution)/shard_map/all_to_all | solution.py:83
  363.7 3.1 copy-start.3
  363.7 4.1 copy-start.7
  367.9 2.1 copy-start.5
  369.9 2.1 copy-start.9
  372.1 4.3 copy-start.11
  372.1 2.2 copy-start.8
  374.3 2.1 copy-start.12
  498.2 192.3 %copy-start.4 = (bf16[512,3456]{1,0:T(8,128)(2,1)S(1)}, bf16[512,3456]{1,0:T(8,128)(2,1)}, u32[]{:S(2)}) copy-start(bf16[512,3456]{1,0:T(8,128)(2,1)} %param.10) | copy-start | bytes 10616836
  498.2 90.1 %all-to-all-start.1 = ((f32[32,208,128]{2,1,0:T(8,128)}), f32[32,208,128]{2,1,0:T(8,128)}, u32[]{:S(2)}, u32[]{:S(2)}) async-start(f32[32,208,128]{2,1,0:T(8,128)} %bitcast.56), calls=%async_computation.1 | async-start | bytes 6815744 | tf_op jit(solution)/shard_map/all_to_all | solution.py:82
  506.1 184.3 %all-reduce.9.cloned.1.call-start = ((), (), s32[]{:S(2)}) async-start(), calls=%async_computation.2 | async-start | bytes 1048576 | tf_op jit(solution)/shard_map/psum | solution.py:90
  585.3 188.6 %all-reduce.13.cloned.1.call-start = ((), (), s32[]{:S(2)}) async-start(), calls=%async_computation.4 | async-start | bytes 3145728 | tf_op jit(solution)/shard_map/psum | solution.py:90
  690.4 232.1 %all-reduce.11.cloned.1.call-start = ((), (), s32[]{:S(2)}) async-start(), calls=%async_computation.3 | async-start | bytes 28311552
  690.5 6.3 copy-start.6
  690.5 6.2 copy-start.10
  701.8 225.9 %copy-start.1 = (bf16[512,3456]{1,0:T(8,128)(2,1)S(1)}, bf16[512,3456]{1,0:T(8,128)(2,1)}, u32[]{:S(2)}) copy-start(bf16[512,3456]{1,0:T(8,128)(2,1)} %param.13) | copy-start | bytes 10616836
Sparse Core Ops, SparseCore 0:
  585.5 104.8 all-reduce.8
  693.5 50.3 all-reduce.12
  749.9 172.6 all-reduce.10
